TPU v7x, 32 devices: a whole 2x2x4 slice. The times are simulated.
32 devices in a mesh: pb: 8 (over y, x, core), dev: 4 (over z).
Axes of the slice: x: 2, y: 2, z: 4, core: 2. Of those that a mesh axis runs over, the one named last changes fastest.
Arguments:
- query_factors: float32 [8192, 128], P('pb'), may hold values from -2.4 to 2.4
- panel_factors: float32 [8192, 128], P(('pb', 'dev')), may hold values from -2.4 to 2.4
- query_weight: float32 [8192], P('pb'), may hold values from 1 to 144, as said below
- plan: int32 [8], replicated, may hold values from 0 to 7, each once
- tile_seeds: int32 [8, 8], replicated, may hold values from 0 to 65520
Outputs:
- query_out: float32 [8192, 128], P('pb')
- panel_out: float32 [8192, 128], P(('pb', 'dev'))
Inputs may be any that keep to these rules, and one draw needn't show every extreme that they name: `query_weight`: each row's weight is positive and at most 144.
All inputs are finite; a program needn't handle non-finite values.
Results may differ from a plain program's by a relative error of at most 0.00018.
Values sent between devices are 32-bit elements; how exact they have to be, the bound alone decides.
No kernel may reach another device: no remote copies, remote signals or barrier semaphores. Data moves between devices by JAX's collectives and lax.ppermute only.
A program may use at most 64 MiB of HBM per device.

v0:
```python
import functools

import jax
import jax.numpy as jnp
from jax import lax
from jax.experimental import pallas as pl
from jax.experimental.pallas import tpu as pltpu
from jax.sharding import PartitionSpec as P

STRATA = 3
epsilon = 1e-06
learning_rate = 0.3


HBM = pl.BlockSpec(memory_space=pltpu.HBM)
VMEM = pl.BlockSpec(memory_space=pltpu.VMEM)
f32, bf16 = jnp.float32, jnp.bfloat16


def dot(a, b):
    return jnp.dot(a, b, preferred_element_type=f32)


def pieces(x):
    hi = x.astype(bf16)
    return hi, (x - hi.astype(f32)).astype(bf16)


def call(kernel, out_shape, operands, *, limit, in_specs=None, scratch=(), flops=0, moved=0):
    return pl.pallas_call(
        kernel,
        out_shape=out_shape,
        in_specs=in_specs or [VMEM] * len(operands),
        out_specs=jax.tree.map(lambda _: VMEM, out_shape),
        scratch_shapes=list(scratch),
        compiler_params=pltpu.CompilerParams(vmem_limit_bytes=limit),
        cost_estimate=pl.CostEstimate(flops=flops, bytes_accessed=moved, transcendentals=0),
    )(*operands)


def wrapped(value):
    return jnp.int32((value + (1 << 31)) % (1 << 32) - (1 << 31))


def hash_block(base, first_ref, second_ref, col, width):
    rows = first_ref.shape[0]
    step = 32
    local_rows = lax.broadcasted_iota(jnp.int32, (step, width), 0)
    local_cols = lax.broadcasted_iota(jnp.int32, (step, width), 1)
    offsets = local_rows * 668265263 + local_cols * 1274126177 + base

    def down(mixed, count):
        return lax.shift_right_logical(mixed, jnp.full(mixed.shape, count, jnp.int32))

    for row in range(0, rows, step):
        mixed = offsets + wrapped(row * 668265263 + col * 1274126177)
        mixed = mixed ^ down(mixed, 15)
        mixed = mixed * 73244475
        mixed = mixed ^ down(mixed, 13)
        mixed = mixed * 1911520717
        mixed = mixed ^ down(mixed, 16)
        first_ref[pl.ds(row, step), pl.ds(col, width)] = (
            (mixed & 65280).astype(f32) - 32768.0
        ).astype(bf16)
        second_ref[pl.ds(row, step), pl.ds(col, width)] = (mixed & 255).astype(f32).astype(bf16)


def step_size(tiles, row, count):
    tile = functools.reduce(jnp.add, [ref[row : row + 8, :] for ref in tiles])
    return learning_rate / jnp.sqrt(
        jnp.sum(tile, axis=(0, 1), keepdims=True) / count + epsilon
    )


def times_gram(left, gram):
    k = gram.shape[0]
    high, low = pieces(gram)
    left_high, left_low = pieces(left)
    packed = jnp.concatenate([left_high, left_low], axis=1)
    wide = jnp.concatenate(
        [
            jnp.concatenate([high, low], axis=1),
            jnp.concatenate([high, jnp.zeros_like(low)], axis=1),
        ],
        axis=0,
    )
    out = dot(packed, wide)
    return out[:, :k] + out[:, k:]


def fold(square):
    k = square.shape[0] // 2
    return square[:k, :k] + (square[:k, k:] + square[k:, :k])


def add_squares(ref, row, block):
    rows, k = block.shape
    ref[row : row + 8, :] += jnp.sum((block * block).reshape(rows // 8, 8, k), axis=0)


def score_strip(packed_ref, first_ref, second_ref, at, *out_refs):
    k = out_refs[0].shape[1]
    out = dot(packed_ref[...], first_ref[:, at]) + dot(packed_ref[...], second_ref[:, at])
    for i, ref in enumerate(out_refs):
        ref[at, :] = (out[2 * i * k : (2 * i + 1) * k] + out[(2 * i + 1) * k : (2 * i + 2) * k]).T


def steps(count, body):
    if count <= 4:
        for j in range(count):
            body(j)
    else:
        lax.fori_loop(0, count, lambda j, _: (body(j), 0)[1], 0)


def score_products(packed_ref, first_ref, second_ref, *out_refs):
    width = 256

    def strip(j):
        at = pl.ds(j * width if isinstance(j, int) else pl.multiple_of(j * width, width), width)
        score_strip(packed_ref, first_ref, second_ref, at, *out_refs)

    steps(first_ref.shape[1] // width, strip)


def across(weight, array):
    return jnp.concatenate(pieces((weight * array).T), axis=0)


def beside(array):
    return jnp.concatenate(pieces(array), axis=1)


down_scale = 1 / 32768


def spread_weight(row_ref, weight_ref):
    strips, k = row_ref.shape
    for i in range(strips):
        weight_ref[i * k : (i + 1) * k, :] = jnp.broadcast_to(row_ref[i : i + 1, :], (k, k)).T


def tile_base(plan_ref, seeds_ref, position, stratum, rows, cols):
    groups = plan_ref.shape[0]
    panel_id = plan_ref[lax.rem(position + (STRATA * groups - stratum), groups)]
    return (
        seeds_ref[position, panel_id] * 374761393
        + (position * rows) * 668265263
        + (panel_id * cols) * 1274126177
    )


def hash_and_products(base, packed_ref, first_ref, second_ref, *out_refs, start=0, held=None):
    width = 256
    for col in range(start, first_ref.shape[1], width):
        hash_block(base, first_ref, second_ref, col, width)
        if held is not None:
            score_strip(*held)
        held = (packed_ref, first_ref, second_ref, pl.ds(col, width), *out_refs)
    return held


def start_kernel(strata, *refs):
    ins, (weight_ref, gram_ref, bases_ref), refs = refs[:4], refs[4:7], refs[7:]
    tiles, refs = refs[: 3 * len(strata)], refs[3 * len(strata) :]
    plan_ref, seeds_ref, factors_ref, row_ref, packed_ref, sem = refs
    copies = [
        pltpu.make_async_copy(src, dst, sem.at[i])
        for i, (src, dst) in enumerate(zip(ins, (plan_ref, seeds_ref, factors_ref, row_ref)))
    ]
    for copy in copies:
        copy.start()
    rows, cols = tiles[0].shape
    position = lax.axis_index("pb")
    groups = plan_ref.shape[0]
    other = lax.rem(position + groups - 1, groups)
    base_of = functools.partial(tile_base, plan_ref, seeds_ref)
    for copy in copies[:2]:
        copy.wait()
    hash_block(base_of(position, strata[0], rows, cols), *tiles[:2], 0, 256)
    for copy in copies[2:]:
        copy.wait()
    spread_weight(row_ref, weight_ref)
    factors = factors_ref[...]
    packed = across(weight_ref[...], factors)
    gram_ref[...] = fold(dot(packed, beside(factors)))
    packed_ref[...] = packed * jnp.asarray(down_scale, bf16)
    lanes = bases_ref.shape[1]
    bases_ref[...] = jnp.zeros_like(bases_ref)
    bases_ref[0:1, :] = jnp.full((1, lanes), base_of(position, STRATA - 1, rows, cols), jnp.int32)
    bases_ref[1:2, :] = jnp.full((1, lanes), base_of(other, 0, rows, cols), jnp.int32)
    held = (packed_ref, *tiles[:2], pl.ds(0, 256), tiles[2])
    for t, first_ref, second_ref, p_ref in zip(strata, tiles[::3], tiles[1::3], tiles[2::3]):
        held = hash_and_products(
            base_of(position, t, rows, cols), packed_ref, first_ref, second_ref, p_ref,
            start=256 if t == strata[0] else 0, held=held,
        )
    score_strip(*held)


def other_kernel(factors_ref, row_ref, bases_ref, p_ref, gram_ref,
                 weight_ref, packed_ref, first_ref, second_ref):
    base = bases_ref[1:2, 0:1]
    hash_block(base, first_ref, second_ref, 0, 256)
    spread_weight(row_ref, weight_ref)
    factors = factors_ref[...]
    packed = across(weight_ref[...], factors)
    gram_ref[...] = fold(dot(packed, beside(factors)))
    packed_ref[...] = packed * jnp.asarray(down_scale, bf16)
    score_strip(*hash_and_products(
        base, packed_ref, first_ref, second_ref, p_ref, start=256,
        held=(packed_ref, first_ref, second_ref, pl.ds(0, 256), p_ref),
    ))


def grad_terms(factors_ref, grad_ref, weight_ref, cross_ref, square_ref, packed_ref):
    packed = across(weight_ref[...], grad_ref[...])
    cross = fold(dot(packed, beside(factors_ref[...])))
    cross_ref[...] = cross + cross.T
    square_ref[...] = fold(dot(packed, beside(grad_ref[...])))
    packed_ref[...] = packed * jnp.asarray(down_scale, bf16)


def grad_kernel(factors_ref, grad_ref, weight_ref, first_ref, second_ref, sums_ref,
                p_ref, cross_ref, square_ref, packed_ref):
    grad_terms(factors_ref, grad_ref, weight_ref, cross_ref, square_ref, packed_ref)
    score_products(packed_ref, first_ref, second_ref, p_ref)


def late_kernel(factors_ref, grad_ref, weight_ref, bases_ref, sums_ref,
                p_ref, cross_ref, square_ref, p_factors_ref, gram_ref, first_ref, second_ref,
                packed_ref):
    k = p_ref.shape[1]
    grad_terms(factors_ref, grad_ref, weight_ref, cross_ref, square_ref, packed_ref.at[: 2 * k])
    other = across(weight_ref[...], factors_ref[...])
    gram_ref[...] = fold(dot(other, beside(factors_ref[...])))
    packed_ref[2 * k :, :] = other * jnp.asarray(down_scale, bf16)
    score_strip(*hash_and_products(
        bases_ref[0:1, 0:1], packed_ref, first_ref, second_ref, p_ref, p_factors_ref
    ))


def panel_side(panel, p, gram, h_ref, squares_ref, packed_ref, panel_gram_ref):
    h = p - times_gram(panel, gram)
    if h_ref is not None:
        h_ref[...] = h
    squares_ref[...] = jnp.zeros_like(squares_ref)
    add_squares(squares_ref, 0, h)
    packed = beside(panel)
    packed_ref[...] = packed * jnp.asarray(down_scale, bf16)
    panel_gram_ref[...] = fold(
        lax.dot_general(packed, packed, (((0,), (0,)), ((), ())), preferred_element_type=f32)
    )


def first_head_kernel(*refs):
    parts, refs = refs[:-7], refs[-7:]
    p_ref, gram_ref, _, panel_ref, squares_ref, packed_ref, panel_gram_ref = refs
    own = lax.axis_index("dev")
    each = parts[0].shape[0]
    for i, part in enumerate(parts):
        place = pl.multiple_of((own ^ i) * each, each) if len(parts) > 1 else 0
        panel_ref[pl.ds(place, each), :] = part[...]
    panel_side(panel_ref[...], p_ref[...], gram_ref[...], None, squares_ref, packed_ref,
               panel_gram_ref)


def carry_kernel(v_count, v_ref, p_ref, gram_ref, *refs):
    tiles, panel_ref = refs[:-1], refs[-1]
    v = v_ref[...]
    panel_ref[...] = v + step_size(tiles, 8, v_count) * (p_ref[...] - times_gram(v, gram_ref[...]))


def head_kernel(last, u_count, v_count, *refs):
    u_before, g_before, v_before, h_before, pu_ref, pg_ref, uu_ref, ug_ref, gg_ref = refs[:9]
    rest = 8 if last else 5
    tiles, refs = refs[9:-rest], refs[-rest:]
    if last:
        factors_ref, v_out, h_out, squares_ref, packed_ref, panel_gram_ref, panel_ref, h_ref = refs
    else:
        factors_ref, h_ref, squares_ref, packed_ref, panel_gram_ref = refs
        panel_ref = v_before
    step = step_size(tiles, 0, u_count)
    factors_ref[...] = u_before[...] + step * g_before[...]
    if last:
        panel_ref[...] = v_before[...] + step_size(tiles, 8, v_count) * h_before[...]
    gram = uu_ref[...] + step * (ug_ref[...] + step * gg_ref[...])
    panel_side(panel_ref[...], pu_ref[...] + step * pg_ref[...], gram, h_ref, squares_ref,
               packed_ref, panel_gram_ref)
    if last:
        each = v_out.shape[0]
        at = pl.ds(pl.multiple_of(lax.axis_index("dev") * each, each), each)
        v_out[...] = panel_ref[at, :]
        h_out[...] = h_ref[at, :]


def tail_kernel(factors_ref, weight_ref, first_ref, second_ref, packed_ref, panel_gram_ref,
                panel_squares_ref, grad_ref, squares_ref):
    rows, k = factors_ref.shape
    squares_ref[:8, :] = jnp.zeros((8, k), f32)
    squares_ref[8:, :] = panel_squares_ref[...]
    panel_gram = panel_gram_ref[...]
    height = 256

    def strip(j):
        at = pl.ds(j * height if isinstance(j, int) else pl.multiple_of(j * height, height), height)
        out = dot(first_ref[at, :], packed_ref[...]) + dot(second_ref[at, :], packed_ref[...])
        g = weight_ref[at, :] * (
            (out[:, :k] + out[:, k:]) - times_gram(factors_ref[at, :], panel_gram)
        )
        grad_ref[at, :] = g
        add_squares(squares_ref, 0, g)

    steps(rows // height, strip)


def last_kernel(u_count, v_count, u_ref, g_ref, v_ref, h_ref, *refs):
    tiles, (u_out, v_out) = refs[:-2], refs[-2:]
    u_out[...] = u_ref[...] + step_size(tiles, 0, u_count) * g_ref[...]
    v_out[...] = v_ref[...] + step_size(tiles, 8, v_count) * h_ref[...]


def shifted(array, axis, by):
    size = lax.axis_size(axis)
    return lax.ppermute(array, axis, [(i, (i + by) % size) for i in range(size)])


def crossed(array, axis, mask):
    return lax.ppermute(array, axis, [(i, i ^ mask) for i in range(lax.axis_size(axis))])


def power_of_two(size):
    return size & (size - 1) == 0


def summands(tile, axis):
    size = lax.axis_size(axis)
    if not power_of_two(size):
        return [lax.psum(tile, axis)]
    tiles, at = [tile], 1
    while at < size:
        tile = functools.reduce(jnp.add, tiles)
        span = 3 if at > 1 and 2 * at < size else 1
        tiles = [tile] + [crossed(tile, axis, at * i) for i in range(1, span + 1)]
        at *= span + 1
    return tiles


def per_device(query_factors, panel_factors, query_weight, plan, tile_seeds):
    groups = lax.axis_size("pb")
    spread = lax.axis_size("dev")
    rows, k = query_factors.shape
    each = panel_factors.shape[0]
    cols = each * spread
    u_count = float(rows * groups * k)
    v_count = float(cols * groups * k)
    shape = jax.ShapeDtypeStruct
    work = 2 * rows * cols * k
    limit = (8 << 20) + (8 if rows * cols <= 1 << 20 else 4) * rows * cols + 28 * k * (rows + cols)
    tile = shape((rows, k), f32)
    whole = shape((cols, k), f32)
    gram_of = shape((k, k), f32)
    pair = [shape((rows, cols), bf16)] * 2
    pack = shape((cols, 2 * k), bf16)
    squares = shape((8, k), f32)
    run = functools.partial(call, limit=limit, moved=4 * rows * cols)

    if spread <= 4 and power_of_two(spread):
        parts = [panel_factors] + [crossed(panel_factors, "dev", i) for i in range(1, spread)]
    else:
        parts = [lax.all_gather(panel_factors, "dev", axis=0, tiled=True)]

    row = query_weight.reshape(rows // k, k)
    factors_by = shifted(query_factors, "pb", 1)
    row_by = shifted(row, "pb", 1)
    across_of = pltpu.VMEM((2 * k, rows), bf16)
    pair_of = [pltpu.VMEM((rows, cols), bf16)] * 2

    def started(strata):
        return run(
            functools.partial(start_kernel, strata),
            [tile, gram_of, shape((8, k), jnp.int32)] + [*pair, whole] * len(strata),
            tuple(pltpu.with_memory_space_constraint(x, pltpu.HBM)
                  for x in (plan, tile_seeds, query_factors, row)),
            in_specs=[HBM] * 4,
            scratch=[pltpu.SMEM(plan.shape, jnp.int32), pltpu.SMEM(tile_seeds.shape, jnp.int32),
                     pltpu.VMEM((rows, k), f32), pltpu.VMEM((rows // k, k), f32),
                     across_of, pltpu.SemaphoreType.DMA((4,))],
            flops=6 * work,
        )

    if rows * cols <= 1 << 20:
        weight, gram, bases, *tiles_of = started([0, 1])
    else:
        weight, gram, bases, *tiles_of = started([0])
        tiles_of += started([1])[3:]
    first, second, p, first_next, second_next, p_factors = tiles_of
    factors = query_factors
    p_by, gram_by = run(
        other_kernel, [whole, gram_of], (factors_by, row_by, bases),
        scratch=[pltpu.VMEM((rows, k), f32), across_of, *pair_of], flops=4 * work,
    )
    panel, panel_squares, packed, panel_gram = run(
        first_head_kernel, [whole, squares, pack, gram_of], (*parts, p, gram, gram_by),
        flops=work // 2,
    )
    for t in range(STRATA):
        last = t == STRATA - 1
        panel = shifted(panel, "pb", 1)
        if t > 0:
            grad_v = shifted(grad_v, "pb", 1)
        grad, sums = run(
            tail_kernel, [tile, shape((16, k), f32)],
            (factors, weight, first, second, packed, panel_gram, panel_squares),
            flops=4 * work,
        )
        tiles = summands(sums, "pb")
        if last:
            break
        outs = [whole, gram_of, gram_of]
        if t == 0:
            first, second = first_next, second_next
            p_grad, cross, square = run(
                grad_kernel, outs, (factors, grad, weight, first, second, sums),
                scratch=[across_of], flops=4 * work,
            )
            (panel,) = run(
                functools.partial(carry_kernel, v_count), [whole],
                (panel, p_by, gram_by, *tiles), flops=work // 8,
            )
            kept, grad_v = [], gram_by
        else:
            p_grad, cross, square, p_factors, gram, first, second = run(
                late_kernel, outs + [whole, gram_of, *pair],
                (factors, grad, weight, bases, sums),
                scratch=[pltpu.VMEM((4 * k, rows), bf16)], flops=8 * work,
            )
            kept = [shape((each, k), f32)]
        ends = t > 0
        factors, *held, grad_v, panel_squares, packed, panel_gram = run(
            functools.partial(head_kernel, ends, u_count, v_count),
            [tile, *kept, kept[0] if ends else whole, squares, pack, gram_of],
            (factors, grad, panel, grad_v, p_factors, p_grad, gram, cross, square, *tiles),
            scratch=[pltpu.VMEM((cols, k), f32)] * (2 if ends else 0), flops=work // 2,
        )
        panel = held[0] if ends else panel
    return run(
        functools.partial(last_kernel, u_count, v_count),
        [tile, shape((each, k), f32)],
        (factors, grad, panel, grad_v, *tiles),
    )


def solution(mesh):
    return jax.shard_map(
        lambda *args: tuple(per_device(*args)),
        mesh=mesh,
        in_specs=(P("pb", None), P(("pb", "dev"), None), P("pb"), P(), P()),
        out_specs=(P("pb", None), P(("pb", "dev"), None)),
        check_vma=False,
    )
```

profile of v0, /device:TPU:0, one launch (start us, length us, event | category | flops | bytes accessed | tf_op | source)
XLA Modules:
  0.0 55.8 jit_solution(12633448777621275397)
XLA Ops:
  0.6 0.5 collective-permute-start.3
  1.2 3.7 %collective-permute-start.1 = (f32[256,128]{1,0:T(8,128)}, f32[256,128]{1,0:T(8,128)S(1)}, u32[]{:S(2)}, u32[]{:S(2)}) collective-permute-start(f32[256,128]{1,0:T(8,128)} %refs_0_.4), channel_id=1, source_target_pairs={{0,2},{1,3},{2,0},{3,1},{4,6},{5,7},{6,4},{7,5},{8,10},{9,11},{10,... | collective-permute-start | bytes 393224 | tf_op jit(solution)/shard_map/ppermute | solution.py:329
  4.8 1.6 %collective-permute-start = (f32[256,128]{1,0:T(8,128)}, f32[256,128]{1,0:T(8,128)S(1)}, u32[]{:S(2)}, u32[]{:S(2)}) collective-permute-start(f32[256,128]{1,0:T(8,128)} %refs_0_.4), channel_id=1, source_target_pairs={{0,1},{1,0},{2,3},{3,2},{4,5},{5,4},{6,7},{7,6},{8,9},{9,8},{10,11... | collective-permute-start | bytes 393224 | tf_op jit(solution)/shard_map/ppermute | solution.py:329
  6.4 0.0 collective-permute-start.2
  6.4 1.0 %collective-permute-start.4 = (f32[8,128]{1,0:T(8,128)}, f32[8,128]{1,0:T(8,128)S(1)}, u32[]{:S(2)}, u32[]{:S(2)}) collective-permute-start(f32[8,128]{1,0:T(8,128)} %bitcast.1), channel_id=1, source_target_pairs={{0,4},{4,8},{8,12},{12,16},{16,20},{20,24},{24,28},{28,0},{1,5},{5... | collective-permute-start | bytes 12296 | tf_op jit(solution)/shard_map/ppermute | solution.py:325
  7.4 6.2 %shard_map.68 = (f32[1024,128]{1,0:T(8,128)S(1)}, f32[128,128]{1,0:T(8,128)S(1)}, s32[8,128]{1,0:T(8,128)S(1)}, bf16[1024,1024]{1,0:T(8,128)(2,1)S(1)}, bf16[102...) custom-call(s32[8]{0:T(128)} %refs_0_.3, ...), custom_call_target="tpu_custom_call" | custom-call | flops 1610612736 | bytes 4194304 | tf_op jit(solution)/shard_map/pallas_call | solution.py:30
  13.5 0.0 copy-start.1
  13.6 0.0 collective-permute-done.4.row_ref
  13.6 0.0 collective-permute-done.3.factors_ref
  13.6 0.0 copy-start
  13.6 2.9 %shard_map.69 = (f32[1024,128]{1,0:T(8,128)S(1)}, f32[128,128]{1,0:T(8,128)S(1)}) custom-call(f32[1024,128]{1,0:T(8,128)S(1)} %collective-permute-done.3.factors_ref, f32[8,128]{1,0:T(8,128)S(1)} %collective-permute-done.4.row_ref, s32[8,128]{1,0:T(8,128)S(1)} %get-tuple-element.49.bases_ref), custom_call_target="tpu_custom_call" | custom-call | flops 1073741824 | bytes 4194304 | tf_op jit(solution)/shard_map/pallas_call | solution.py:30
  16.5 0.0 collective-permute-done.1.refs_2_
  16.5 0.0 collective-permute-done.refs_1_
  16.5 0.0 collective-permute-done.2.refs_3_
  16.5 0.0 copy-done.1
  16.5 0.5 shard_map.70
  17.0 0.9 %collective-permute-start.5 = (f32[1024,128]{1,0:T(8,128)S(1)}, f32[1024,128]{1,0:T(8,128)S(1)}, u32[]{:S(2)}, u32[]{:S(2)}) collective-permute-start(f32[1024,128]{1,0:T(8,128)S(1)} %get-tuple-element.55), channel_id=1, source_target_pairs={{0,4},{4,8},{8,12},{12,16},{16,20},{20,24},{24,28},{28,0},{1,5},{5... | collective-permute-start | bytes 1572872 | tf_op jit(solution)/shard_map/ppermute | solution.py:325
  17.9 0.0 copy-done
  17.9 1.4 %shard_map.71 = (f32[1024,128]{1,0:T(8,128)S(1)}, f32[16,128]{1,0:T(8,128)S(1)}) custom-call(f32[1024,128]{1,0:T(8,128)S(1)} %copy-done, f32[1024,128]{1,0:T(8,128)S(1)} %get-tuple-element.44.weight_ref, bf16[1024,1024]{1,0:T(8,128)(2,1)S(1)} %get-tuple-element.45.first_ref, bf16[1024,1024]{1,0:T(8,128)(2,1)S(1)} %get-tuple-element.46.second_ref, ...), custom_call_target="tpu_custom_call" | custom-call | flops 1073741824 | bytes 4194304 | tf_op jit(solution)/shard_map/pallas_call | solution.py:30
  19.3 0.8 %collective-permute-start.6 = (f32[16,128]{1,0:T(8,128)S(1)}, f32[16,128]{1,0:T(8,128)S(1)}, u32[]{:S(2)}, u32[]{:S(2)}) collective-permute-start(f32[16,128]{1,0:T(8,128)S(1)} %get-tuple-element.57.sums_ref), channel_id=1, source_target_pairs={{0,4},{4,0},{8,12},{12,8},{16,20},{20,16},{24,28},{28,24},{1,5},{5... | collective-permute-start | bytes 24584 | tf_op jit(solution)/shard_map/ppermute | solution.py:329
  20.2 0.8 %collective-permute-done.6 = f32[16,128]{1,0:T(8,128)S(1)} collective-permute-done((f32[16,128]{1,0:T(8,128)S(1)}, f32[16,128]{1,0:T(8,128)S(1)}, u32[]{:S(2)}, u32[]{:S(2)}) %collective-permute-start.6) | collective-permute-done | bytes 8224 | tf_op jit(solution)/shard_map/ppermute | solution.py:329
  21.0 1.4 %collective-permute-start.9 = (f32[16,128]{1,0:T(8,128)S(1)}, f32[16,128]{1,0:T(8,128)S(1)}, u32[]{:S(2)}, u32[]{:S(2)}) collective-permute-start(f32[16,128]{1,0:T(8,128)S(1)} %add.9.refs_0_.refs_9_), channel_id=1, source_target_pairs={{0,24},{4,28},{8,16},{12,20},{16,8},{20,12},{24,0},{28,4},{1,25},{... | collective-permute-start | bytes 24584 | tf_op jit(solution)/shard_map/ppermute | solution.py:329
  22.4 1.5 %collective-permute-start.8 = (f32[16,128]{1,0:T(8,128)S(1)}, f32[16,128]{1,0:T(8,128)S(1)}, u32[]{:S(2)}, u32[]{:S(2)}) collective-permute-start(f32[16,128]{1,0:T(8,128)S(1)} %add.9.refs_0_.refs_9_), channel_id=1, source_target_pairs={{0,16},{4,20},{8,24},{12,28},{16,0},{20,4},{24,8},{28,12},{1,17},{... | collective-permute-start | bytes 24584 | tf_op jit(solution)/shard_map/ppermute | solution.py:329
  24.0 0.5 collective-permute-start.7
  24.5 1.7 %shard_map.73 = (f32[1024,128]{1,0:T(8,128)S(1)}, f32[128,128]{1,0:T(8,128)S(1)}, f32[128,128]{1,0:T(8,128)S(1)}) custom-call(f32[1024,128]{1,0:T(8,128)S(1)} %copy-done, f32[1024,128]{1,0:T(8,128)S(1)} %get-tuple-element.54.grad_ref.refs_1_, f32[1024,128]{1,0:T(8,128)S(1)} %get-tuple-element.44.weight_ref, ...), custom_call_target="tpu_custom_call" | custom-call | flops 1073741824 | bytes 4194304 | tf_op jit(solution)/shard_map/pallas_call | solution.py:30
  26.2 0.0 collective-permute-done.9.refs_3_.refs_12_
  26.2 0.7 %collective-permute-done.8.refs_2_.refs_11_ = f32[16,128]{1,0:T(8,128)S(1)} collective-permute-done((f32[16,128]{1,0:T(8,128)S(1)}, f32[16,128]{1,0:T(8,128)S(1)}, u32[]{:S(2)}, u32[]{:S(2)}) %collective-permute-start.8) | collective-permute-done | bytes 8224 | tf_op jit(solution)/shard_map/ppermute | solution.py:329
  26.9 0.7 %collective-permute-done.7.refs_1_.refs_10_ = f32[16,128]{1,0:T(8,128)S(1)} collective-permute-done((f32[16,128]{1,0:T(8,128)S(1)}, f32[16,128]{1,0:T(8,128)S(1)}, u32[]{:S(2)}, u32[]{:S(2)}) %collective-permute-start.7) | collective-permute-done | bytes 8224 | tf_op jit(solution)/shard_map/ppermute | solution.py:329
  27.6 0.0 collective-permute-done.5.v_ref
  27.6 0.3 shard_map.72.refs_2_
  27.9 0.2 collective-permute-start.10
  28.2 0.7 %shard_map.74 = (f32[1024,128]{1,0:T(8,128)S(1)}, f32[1024,128]{1,0:T(8,128)S(1)}, f32[8,128]{1,0:T(8,128)S(1)}, bf16[1024,256]{1,0:T(8,128)(2,1)S(1)}, f32[128,128]{1,0:T(8,128)S(1)}) custom-call(f32[1024,128]{1,0:T(8,128)S(1)} %copy-done, f32[1024,128]{1,0:T(8,128)S(1)} %get-tuple-element.54.grad_ref.refs_1_, f32[1024,128]{1,0:T(8,128)S(1)} %shard_map.72.refs_2_, ...), custom_call_target="tpu_custom_call" | custom-call | flops 134217728 | bytes 4194304 | tf_op jit(solution)/shard_map/pallas_call | solution.py:30
  28.9 0.7 %collective-permute-start.11 = (f32[1024,128]{1,0:T(8,128)S(1)}, f32[1024,128]{1,0:T(8,128)S(1)}, u32[]{:S(2)}, u32[]{:S(2)}) collective-permute-start(f32[1024,128]{1,0:T(8,128)S(1)} %get-tuple-element.69), channel_id=1, source_target_pairs={{0,4},{4,8},{8,12},{12,16},{16,20},{20,24},{24,28},{28,0},{1,5},{5... | collective-permute-start | bytes 1572872 | tf_op jit(solution)/shard_map/ppermute | solution.py:325
  29.6 1.4 %shard_map.75 = (f32[1024,128]{1,0:T(8,128)S(1)}, f32[16,128]{1,0:T(8,128)S(1)}) custom-call(f32[1024,128]{1,0:T(8,128)S(1)} %get-tuple-element.64.factors_ref.refs_0_, f32[1024,128]{1,0:T(8,128)S(1)} %get-tuple-element.44.weight_ref, bf16[1024,1024]{1,0:T(8,128)(2,1)S(1)} %get-tuple-element.59.first_ref, ...), custom_call_target="tpu_custom_call" | custom-call | flops 1073741824 | bytes 4194304 | tf_op jit(solution)/shard_map/pallas_call | solution.py:30
  31.0 0.1 collective-permute-start.12
  31.1 1.2 %collective-permute-done.12 = f32[16,128]{1,0:T(8,128)S(1)} collective-permute-done((f32[16,128]{1,0:T(8,128)S(1)}, f32[16,128]{1,0:T(8,128)S(1)}, u32[]{:S(2)}, u32[]{:S(2)}) %collective-permute-start.12) | collective-permute-done | bytes 8224 | tf_op jit(solution)/shard_map/ppermute | solution.py:329
  32.2 2.4 %collective-permute-start.15 = (f32[16,128]{1,0:T(8,128)S(1)}, f32[16,128]{1,0:T(8,128)S(1)}, u32[]{:S(2)}, u32[]{:S(2)}) collective-permute-start(f32[16,128]{1,0:T(8,128)S(1)} %add.10.refs_9_), channel_id=1, source_target_pairs={{0,24},{4,28},{8,16},{12,20},{16,8},{20,12},{24,0},{28,4},{1,25},{... | collective-permute-start | bytes 24584 | tf_op jit(solution)/shard_map/ppermute | solution.py:329
  34.6 0.8 %collective-permute-start.14 = (f32[16,128]{1,0:T(8,128)S(1)}, f32[16,128]{1,0:T(8,128)S(1)}, u32[]{:S(2)}, u32[]{:S(2)}) collective-permute-start(f32[16,128]{1,0:T(8,128)S(1)} %add.10.refs_9_), channel_id=1, source_target_pairs={{0,16},{4,20},{8,24},{12,28},{16,0},{20,4},{24,8},{28,12},{1,17},{... | collective-permute-start | bytes 24584 | tf_op jit(solution)/shard_map/ppermute | solution.py:329
  35.5 0.3 collective-permute-start.13
  35.7 3.4 %shard_map.76 = (f32[1024,128]{1,0:T(8,128)S(1)}, f32[128,128]{1,0:T(8,128)S(1)}, f32[128,128]{1,0:T(8,128)S(1)}, f32[1024,128]{1,0:T(8,128)S(1)}, f32[128,128]{...) custom-call(f32[1024,128]{1,0:T(8,128)S(1)} %get-tuple-element.64.factors_ref.refs_0_, ...), custom_call_target="tpu_custom_call" | custom-call | flops 2147483648 | bytes 4194304 | tf_op jit(solution)/shard_map/pallas_call | solution.py:30
  39.1 0.0 collective-permute-done.15.refs_12_
  39.1 4.6 %collective-permute-done.14.refs_11_ = f32[16,128]{1,0:T(8,128)S(1)} collective-permute-done((f32[16,128]{1,0:T(8,128)S(1)}, f32[16,128]{1,0:T(8,128)S(1)}, u32[]{:S(2)}, u32[]{:S(2)}) %collective-permute-start.14) | collective-permute-done | bytes 8224 | tf_op jit(solution)/shard_map/ppermute | solution.py:329
  43.7 0.0 collective-permute-done.13.refs_10_
  43.7 0.0 collective-permute-done.10.refs_2_
  43.7 0.0 collective-permute-done.11.refs_3_
  43.7 0.8 %shard_map.77 = (f32[1024,128]{1,0:T(8,128)S(1)}, f32[256,128]{1,0:T(8,128)S(1)}, f32[256,128]{1,0:T(8,128)S(1)}, f32[8,128]{1,0:T(8,128)S(1)}, bf16[1024,256]{1,0:T(8,128)(2,1)S(1)}, /*index=5*/f32[128,128]{1,0:T(8,128)S(1)}) custom-call(f32[1024,128]{1,0:T(8,128)S(1)} %get-tuple-element.64.factors_ref.refs_0_, ...), custom_call_target="tpu_custom_call" | custom-call | flops 134217728 | bytes 4194304 | tf_op jit(solution)/shard_map/pallas_call | solution.py:30
  44.5 0.1 collective-permute-start.16
  44.5 0.1 collective-permute-start.17
  44.6 1.5 %shard_map.78 = (f32[1024,128]{1,0:T(8,128)S(1)}, f32[16,128]{1,0:T(8,128)S(1)}) custom-call(f32[1024,128]{1,0:T(8,128)S(1)} %get-tuple-element.76.factors_ref.u_ref, f32[1024,128]{1,0:T(8,128)S(1)} %get-tuple-element.44.weight_ref, bf16[1024,1024]{1,0:T(8,128)(2,1)S(1)} %get-tuple-element.77.first_ref, bf16[1024,1024]{1,0:T(8,128)(2,1)S(1)} %get-tuple-element.78.second_ref, ...), custom_call_target="tpu_custom_call" | custom-call | flops 1073741824 | bytes 4194304 | tf_op jit(solution)/shard_map/pallas_call | solution.py:30
  46.1 0.1 collective-permute-start.18
  46.2 1.2 %collective-permute-done.18 = f32[16,128]{1,0:T(8,128)S(1)} collective-permute-done((f32[16,128]{1,0:T(8,128)S(1)}, f32[16,128]{1,0:T(8,128)S(1)}, u32[]{:S(2)}, u32[]{:S(2)}) %collective-permute-start.18) | collective-permute-done | bytes 8224 | tf_op jit(solution)/shard_map/ppermute | solution.py:329
  47.3 3.0 %collective-permute-start.21 = (f32[16,128]{1,0:T(8,128)S(1)}, f32[16,128]{1,0:T(8,128)S(1)}, u32[]{:S(2)}, u32[]{:S(2)}) collective-permute-start(f32[16,128]{1,0:T(8,128)S(1)} %add.11.refs_0_), channel_id=1, source_target_pairs={{0,24},{4,28},{8,16},{12,20},{16,8},{20,12},{24,0},{28,4},{1,25},{... | collective-permute-start | bytes 24584 | tf_op jit(solution)/shard_map/ppermute | solution.py:329
  50.3 0.8 %collective-permute-start.20 = (f32[16,128]{1,0:T(8,128)S(1)}, f32[16,128]{1,0:T(8,128)S(1)}, u32[]{:S(2)}, u32[]{:S(2)}) collective-permute-start(f32[16,128]{1,0:T(8,128)S(1)} %add.11.refs_0_), channel_id=1, source_target_pairs={{0,16},{4,20},{8,24},{12,28},{16,0},{20,4},{24,8},{28,12},{1,17},{... | collective-permute-start | bytes 24584 | tf_op jit(solution)/shard_map/ppermute | solution.py:329
  51.1 0.0 collective-permute-start.19
  51.1 0.8 %collective-permute-done.21.refs_3_ = f32[16,128]{1,0:T(8,128)S(1)} collective-permute-done((f32[16,128]{1,0:T(8,128)S(1)}, f32[16,128]{1,0:T(8,128)S(1)}, u32[]{:S(2)}, u32[]{:S(2)}) %collective-permute-start.21) | collective-permute-done | bytes 8224 | tf_op jit(solution)/shard_map/ppermute | solution.py:329
  51.9 2.0 %collective-permute-done.20.refs_2_ = f32[16,128]{1,0:T(8,128)S(1)} collective-permute-done((f32[16,128]{1,0:T(8,128)S(1)}, f32[16,128]{1,0:T(8,128)S(1)}, u32[]{:S(2)}, u32[]{:S(2)}) %collective-permute-start.20) | collective-permute-done | bytes 8224 | tf_op jit(solution)/shard_map/ppermute | solution.py:329
  53.9 0.8 %collective-permute-done.19.refs_1_ = f32[16,128]{1,0:T(8,128)S(1)} collective-permute-done((f32[16,128]{1,0:T(8,128)S(1)}, f32[16,128]{1,0:T(8,128)S(1)}, u32[]{:S(2)}, u32[]{:S(2)}) %collective-permute-start.19) | collective-permute-done | bytes 8224 | tf_op jit(solution)/shard_map/ppermute | solution.py:329
  54.8 0.0 collective-permute-done.16.v_ref
  54.8 0.0 collective-permute-done.17.h_ref
  54.8 1.0 %shard_map.79 = (f32[1024,128]{1,0:T(8,128)}, f32[256,128]{1,0:T(8,128)}) custom-call(f32[1024,128]{1,0:T(8,128)S(1)} %get-tuple-element.76.factors_ref.u_ref, f32[1024,128]{1,0:T(8,128)S(1)} %get-tuple-element.82.g_ref, f32[256,128]{1,0:T(8,128)S(1)} %collective-permute-done.16.v_ref, f32[256,128]{1,0:T(8,128)S(1)} %collective-permute-done.17.h_ref, ...), custom_call_target="tpu_custom_call" | custom-call | bytes 4194304 | tf_op jit(solution)/shard_map/pallas_call | solution.py:30
  (3 shorter events, 0.0 us)
Async XLA Ops:
  0.6 12.9 %collective-permute-start.3 = (f32[1024,128]{1,0:T(8,128)}, f32[1024,128]{1,0:T(8,128)S(1)}, u32[]{:S(2)}, u32[]{:S(2)}) collective-permute-start(f32[1024,128]{1,0:T(8,128)} %refs_0_.5), channel_id=1, source_target_pairs={{0,4},{4,8},{8,12},{12,16},{16,20},{20,24},{24,28},{28,0},{1,5},{5... | collective-permute-start | bytes 1572872 | tf_op jit(solution)/shard_map/ppermute | solution.py:325
  1.2 15.3 %collective-permute-start.1 = (f32[256,128]{1,0:T(8,128)}, f32[256,128]{1,0:T(8,128)S(1)}, u32[]{:S(2)}, u32[]{:S(2)}) collective-permute-start(f32[256,128]{1,0:T(8,128)} %refs_0_.4), channel_id=1, source_target_pairs={{0,2},{1,3},{2,0},{3,1},{4,6},{5,7},{6,4},{7,5},{8,10},{9,11},{10,... | collective-permute-start | bytes 393224 | tf_op jit(solution)/shard_map/ppermute | solution.py:329
  4.8 11.7 %collective-permute-start = (f32[256,128]{1,0:T(8,128)}, f32[256,128]{1,0:T(8,128)S(1)}, u32[]{:S(2)}, u32[]{:S(2)}) collective-permute-start(f32[256,128]{1,0:T(8,128)} %refs_0_.4), channel_id=1, source_target_pairs={{0,1},{1,0},{2,3},{3,2},{4,5},{5,4},{6,7},{7,6},{8,9},{9,8},{10,11... | collective-permute-start | bytes 393224 | tf_op jit(solution)/shard_map/ppermute | solution.py:329
  6.4 10.1 %collective-permute-start.2 = (f32[256,128]{1,0:T(8,128)}, f32[256,128]{1,0:T(8,128)S(1)}, u32[]{:S(2)}, u32[]{:S(2)}) collective-permute-start(f32[256,128]{1,0:T(8,128)} %refs_0_.4), channel_id=1, source_target_pairs={{0,3},{1,2},{2,1},{3,0},{4,7},{5,6},{6,5},{7,4},{8,11},{9,10},{10,... | collective-permute-start | bytes 393224 | tf_op jit(solution)/shard_map/ppermute | solution.py:329
  6.4 7.2 %collective-permute-start.4 = (f32[8,128]{1,0:T(8,128)}, f32[8,128]{1,0:T(8,128)S(1)}, u32[]{:S(2)}, u32[]{:S(2)}) collective-permute-start(f32[8,128]{1,0:T(8,128)} %bitcast.1), channel_id=1, source_target_pairs={{0,4},{4,8},{8,12},{12,16},{16,20},{20,24},{24,28},{28,0},{1,5},{5... | collective-permute-start | bytes 12296 | tf_op jit(solution)/shard_map/ppermute | solution.py:325
  13.5 3.0 %copy-start.1 = (f32[256,128]{1,0:T(8,128)S(1)}, f32[256,128]{1,0:T(8,128)}, u32[]{:S(2)}) copy-start(f32[256,128]{1,0:T(8,128)} %refs_0_.4) | copy-start | bytes 393220
  13.6 4.3 %copy-start = (f32[1024,128]{1,0:T(8,128)S(1)}, f32[1024,128]{1,0:T(8,128)}, u32[]{:S(2)}) copy-start(f32[1024,128]{1,0:T(8,128)} %refs_0_.5) | copy-start | bytes 1572868
  17.0 10.6 %collective-permute-start.5 = (f32[1024,128]{1,0:T(8,128)S(1)}, f32[1024,128]{1,0:T(8,128)S(1)}, u32[]{:S(2)}, u32[]{:S(2)}) collective-permute-start(f32[1024,128]{1,0:T(8,128)S(1)} %get-tuple-element.55), channel_id=1, source_target_pairs={{0,4},{4,8},{8,12},{12,16},{16,20},{20,24},{24,28},{28,0},{1,5},{5... | collective-permute-start | bytes 1572872 | tf_op jit(solution)/shard_map/ppermute | solution.py:325
  19.3 1.7 %collective-permute-start.6 = (f32[16,128]{1,0:T(8,128)S(1)}, f32[16,128]{1,0:T(8,128)S(1)}, u32[]{:S(2)}, u32[]{:S(2)}) collective-permute-start(f32[16,128]{1,0:T(8,128)S(1)} %get-tuple-element.57.sums_ref), channel_id=1, source_target_pairs={{0,4},{4,0},{8,12},{12,8},{16,20},{20,16},{24,28},{28,24},{1,5},{5... | collective-permute-start | bytes 24584 | tf_op jit(solution)/shard_map/ppermute | solution.py:329
  21.0 5.2 %collective-permute-start.9 = (f32[16,128]{1,0:T(8,128)S(1)}, f32[16,128]{1,0:T(8,128)S(1)}, u32[]{:S(2)}, u32[]{:S(2)}) collective-permute-start(f32[16,128]{1,0:T(8,128)S(1)} %add.9.refs_0_.refs_9_), channel_id=1, source_target_pairs={{0,24},{4,28},{8,16},{12,20},{16,8},{20,12},{24,0},{28,4},{1,25},{... | collective-permute-start | bytes 24584 | tf_op jit(solution)/shard_map/ppermute | solution.py:329
  22.4 4.5 %collective-permute-start.8 = (f32[16,128]{1,0:T(8,128)S(1)}, f32[16,128]{1,0:T(8,128)S(1)}, u32[]{:S(2)}, u32[]{:S(2)}) collective-permute-start(f32[16,128]{1,0:T(8,128)S(1)} %add.9.refs_0_.refs_9_), channel_id=1, source_target_pairs={{0,16},{4,20},{8,24},{12,28},{16,0},{20,4},{24,8},{28,12},{1,17},{... | collective-permute-start | bytes 24584 | tf_op jit(solution)/shard_map/ppermute | solution.py:329
  24.0 3.7 %collective-permute-start.7 = (f32[16,128]{1,0:T(8,128)S(1)}, f32[16,128]{1,0:T(8,128)S(1)}, u32[]{:S(2)}, u32[]{:S(2)}) collective-permute-start(f32[16,128]{1,0:T(8,128)S(1)} %add.9.refs_0_.refs_9_), channel_id=1, source_target_pairs={{0,8},{4,12},{8,0},{12,4},{16,24},{20,28},{24,16},{28,20},{1,9},{5... | collective-permute-start | bytes 24584 | tf_op jit(solution)/shard_map/ppermute | solution.py:329
  27.9 15.7 %collective-permute-start.10 = (f32[1024,128]{1,0:T(8,128)S(1)}, f32[1024,128]{1,0:T(8,128)S(1)}, u32[]{:S(2)}, u32[]{:S(2)}) collective-permute-start(f32[1024,128]{1,0:T(8,128)S(1)} %shard_map.72.refs_2_), channel_id=1, source_target_pairs={{0,4},{4,8},{8,12},{12,16},{16,20},{20,24},{24,28},{28,0},{1,5},{5... | collective-permute-start | bytes 1572872 | tf_op jit(solution)/shard_map/ppermute | solution.py:325
  28.9 14.8 %collective-permute-start.11 = (f32[1024,128]{1,0:T(8,128)S(1)}, f32[1024,128]{1,0:T(8,128)S(1)}, u32[]{:S(2)}, u32[]{:S(2)}) collective-permute-start(f32[1024,128]{1,0:T(8,128)S(1)} %get-tuple-element.69), channel_id=1, source_target_pairs={{0,4},{4,8},{8,12},{12,16},{16,20},{20,24},{24,28},{28,0},{1,5},{5... | collective-permute-start | bytes 1572872 | tf_op jit(solution)/shard_map/ppermute | solution.py:325
  31.0 1.2 %collective-permute-start.12 = (f32[16,128]{1,0:T(8,128)S(1)}, f32[16,128]{1,0:T(8,128)S(1)}, u32[]{:S(2)}, u32[]{:S(2)}) collective-permute-start(f32[16,128]{1,0:T(8,128)S(1)} %get-tuple-element.70.sums_ref), channel_id=1, source_target_pairs={{0,4},{4,0},{8,12},{12,8},{16,20},{20,16},{24,28},{28,24},{1,5},{5... | collective-permute-start | bytes 24584 | tf_op jit(solution)/shard_map/ppermute | solution.py:329
  32.2 6.9 %collective-permute-start.15 = (f32[16,128]{1,0:T(8,128)S(1)}, f32[16,128]{1,0:T(8,128)S(1)}, u32[]{:S(2)}, u32[]{:S(2)}) collective-permute-start(f32[16,128]{1,0:T(8,128)S(1)} %add.10.refs_9_), channel_id=1, source_target_pairs={{0,24},{4,28},{8,16},{12,20},{16,8},{20,12},{24,0},{28,4},{1,25},{... | collective-permute-start | bytes 24584 | tf_op jit(solution)/shard_map/ppermute | solution.py:329
  34.6 9.0 %collective-permute-start.14 = (f32[16,128]{1,0:T(8,128)S(1)}, f32[16,128]{1,0:T(8,128)S(1)}, u32[]{:S(2)}, u32[]{:S(2)}) collective-permute-start(f32[16,128]{1,0:T(8,128)S(1)} %add.10.refs_9_), channel_id=1, source_target_pairs={{0,16},{4,20},{8,24},{12,28},{16,0},{20,4},{24,8},{28,12},{1,17},{... | collective-permute-start | bytes 24584 | tf_op jit(solution)/shard_map/ppermute | solution.py:329
  35.5 8.2 %collective-permute-start.13 = (f32[16,128]{1,0:T(8,128)S(1)}, f32[16,128]{1,0:T(8,128)S(1)}, u32[]{:S(2)}, u32[]{:S(2)}) collective-permute-start(f32[16,128]{1,0:T(8,128)S(1)} %add.10.refs_9_), channel_id=1, source_target_pairs={{0,8},{4,12},{8,0},{12,4},{16,24},{20,28},{24,16},{28,20},{1,9},{5... | collective-permute-start | bytes 24584 | tf_op jit(solution)/shard_map/ppermute | solution.py:329
  44.5 10.3 %collective-permute-start.16 = (f32[256,128]{1,0:T(8,128)S(1)}, f32[256,128]{1,0:T(8,128)S(1)}, u32[]{:S(2)}, u32[]{:S(2)}) collective-permute-start(f32[256,128]{1,0:T(8,128)S(1)} %get-tuple-element.83), channel_id=1, source_target_pairs={{0,4},{4,8},{8,12},{12,16},{16,20},{20,24},{24,28},{28,0},{1,5},{5... | collective-permute-start | bytes 393224 | tf_op jit(solution)/shard_map/ppermute | solution.py:325
  44.5 10.2 %collective-permute-start.17 = (f32[256,128]{1,0:T(8,128)S(1)}, f32[256,128]{1,0:T(8,128)S(1)}, u32[]{:S(2)}, u32[]{:S(2)}) collective-permute-start(f32[256,128]{1,0:T(8,128)S(1)} %get-tuple-element.84), channel_id=1, source_target_pairs={{0,4},{4,8},{8,12},{12,16},{16,20},{20,24},{24,28},{28,0},{1,5},{5... | collective-permute-start | bytes 393224 | tf_op jit(solution)/shard_map/ppermute | solution.py:325
  46.1 1.2 %collective-permute-start.18 = (f32[16,128]{1,0:T(8,128)S(1)}, f32[16,128]{1,0:T(8,128)S(1)}, u32[]{:S(2)}, u32[]{:S(2)}) collective-permute-start(f32[16,128]{1,0:T(8,128)S(1)} %get-tuple-element.85), channel_id=1, source_target_pairs={{0,4},{4,0},{8,12},{12,8},{16,20},{20,16},{24,28},{28,24},{1,5},{5... | collective-permute-start | bytes 24584 | tf_op jit(solution)/shard_map/ppermute | solution.py:329
  47.3 4.6 %collective-permute-start.21 = (f32[16,128]{1,0:T(8,128)S(1)}, f32[16,128]{1,0:T(8,128)S(1)}, u32[]{:S(2)}, u32[]{:S(2)}) collective-permute-start(f32[16,128]{1,0:T(8,128)S(1)} %add.11.refs_0_), channel_id=1, source_target_pairs={{0,24},{4,28},{8,16},{12,20},{16,8},{20,12},{24,0},{28,4},{1,25},{... | collective-permute-start | bytes 24584 | tf_op jit(solution)/shard_map/ppermute | solution.py:329
  50.3 3.7 %collective-permute-start.20 = (f32[16,128]{1,0:T(8,128)S(1)}, f32[16,128]{1,0:T(8,128)S(1)}, u32[]{:S(2)}, u32[]{:S(2)}) collective-permute-start(f32[16,128]{1,0:T(8,128)S(1)} %add.11.refs_0_), channel_id=1, source_target_pairs={{0,16},{4,20},{8,24},{12,28},{16,0},{20,4},{24,8},{28,12},{1,17},{... | collective-permute-start | bytes 24584 | tf_op jit(solution)/shard_map/ppermute | solution.py:329
  51.1 3.7 %collective-permute-start.19 = (f32[16,128]{1,0:T(8,128)S(1)}, f32[16,128]{1,0:T(8,128)S(1)}, u32[]{:S(2)}, u32[]{:S(2)}) collective-permute-start(f32[16,128]{1,0:T(8,128)S(1)} %add.11.refs_0_), channel_id=1, source_target_pairs={{0,8},{4,12},{8,0},{12,4},{16,24},{20,28},{24,16},{28,20},{1,9},{5... | collective-permute-start | bytes 24584 | tf_op jit(solution)/shard_map/ppermute | solution.py:329
where the time goes:
time: 56.1 us; the launch traced here: 55.8 us
  Pallas kernels  21.8 us (39%)
  starting transfers between devices  20.4 us (36%)
  waiting for transfers between devices  12.8 us (23%)
  between operations  0.83 us (1%)
    pallas_call x12, Pallas kernels, call(): pl.pallas_call(kernel, out_shape=out_shape, in_specs=in_specs or [VMEM] *...  21.8 us
    ppermute x15, starting transfers between devices, crossed(): lax.ppermute(array, axis, [(i, i ^ mask) for i in range(lax.axis_size(axi...  17 us
    ppermute x15, waiting for transfers between devices, crossed(): lax.ppermute(array, axis, [(i, i ^ mask) for i in range(lax.axis_size(axi...  12.8 us
    ppermute x7, starting transfers between devices, shifted(): lax.ppermute(array, axis, [(i, (i + by) % size) for i in range(size)])  3.43 us
  transfers between devices with their start and end apart: 22, of which 9 were waited for; matrix products, arithmetic and copies ran while one was open for 0% of the time, Pallas kernels for 34%

commit v1 on v0

--- a/solution.py
+++ b/solution.py
@@ -273,10 +273,10 @@
 
 def head_kernel(last, u_count, v_count, *refs):
     u_before, g_before, v_before, h_before, pu_ref, pg_ref, uu_ref, ug_ref, gg_ref = refs[:9]
-    rest = 8 if last else 5
+    rest = 7 if last else 5
     tiles, refs = refs[9:-rest], refs[-rest:]
     if last:
-        factors_ref, v_out, h_out, squares_ref, packed_ref, panel_gram_ref, panel_ref, h_ref = refs
+        factors_ref, out_ref, squares_ref, packed_ref, panel_gram_ref, panel_ref, h_ref = refs
     else:
         factors_ref, h_ref, squares_ref, packed_ref, panel_gram_ref = refs
         panel_ref = v_before
@@ -288,10 +288,10 @@
     panel_side(panel_ref[...], pu_ref[...] + step * pg_ref[...], gram, h_ref, squares_ref,
                packed_ref, panel_gram_ref)
     if last:
-        each = v_out.shape[0]
+        each = out_ref.shape[0] // 2
         at = pl.ds(pl.multiple_of(lax.axis_index("dev") * each, each), each)
-        v_out[...] = panel_ref[at, :]
-        h_out[...] = h_ref[at, :]
+        out_ref[:each, :] = panel_ref[at, :]
+        out_ref[each:, :] = h_ref[at, :]
 
 
 def tail_kernel(factors_ref, weight_ref, first_ref, second_ref, packed_ref, panel_gram_ref,
@@ -314,10 +314,11 @@
     steps(rows // height, strip)
 
 
-def last_kernel(u_count, v_count, u_ref, g_ref, v_ref, h_ref, *refs):
+def last_kernel(u_count, v_count, u_ref, g_ref, both_ref, *refs):
     tiles, (u_out, v_out) = refs[:-2], refs[-2:]
     u_out[...] = u_ref[...] + step_size(tiles, 0, u_count) * g_ref[...]
-    v_out[...] = v_ref[...] + step_size(tiles, 8, v_count) * h_ref[...]
+    each = v_out.shape[0]
+    v_out[...] = both_ref[:each, :] + step_size(tiles, 8, v_count) * both_ref[each:, :]
 
 
 def shifted(array, axis, by):
@@ -407,7 +408,7 @@
     for t in range(STRATA):
         last = t == STRATA - 1
         panel = shifted(panel, "pb", 1)
-        if t > 0:
+        if 0 < t < STRATA - 1:
             grad_v = shifted(grad_v, "pb", 1)
         grad, sums = run(
             tail_kernel, [tile, shape((16, k), f32)],
@@ -428,26 +429,28 @@
                 functools.partial(carry_kernel, v_count), [whole],
                 (panel, p_by, gram_by, *tiles), flops=work // 8,
             )
-            kept, grad_v = [], gram_by
+            grad_v = gram_by
         else:
             p_grad, cross, square, p_factors, gram, first, second = run(
                 late_kernel, outs + [whole, gram_of, *pair],
                 (factors, grad, weight, bases, sums),
                 scratch=[pltpu.VMEM((4 * k, rows), bf16)], flops=8 * work,
             )
-            kept = [shape((each, k), f32)]
         ends = t > 0
-        factors, *held, grad_v, panel_squares, packed, panel_gram = run(
+        factors, moving, panel_squares, packed, panel_gram = run(
             functools.partial(head_kernel, ends, u_count, v_count),
-            [tile, *kept, kept[0] if ends else whole, squares, pack, gram_of],
+            [tile, shape((2 * each, k), f32) if ends else whole, squares, pack, gram_of],
             (factors, grad, panel, grad_v, p_factors, p_grad, gram, cross, square, *tiles),
             scratch=[pltpu.VMEM((cols, k), f32)] * (2 if ends else 0), flops=work // 2,
         )
-        panel = held[0] if ends else panel
+        if ends:
+            panel = moving
+        else:
+            grad_v = moving
     return run(
         functools.partial(last_kernel, u_count, v_count),
         [tile, shape((each, k), f32)],
-        (factors, grad, panel, grad_v, *tiles),
+        (factors, grad, panel, *tiles),
     )
 
 

time: 56.1 us -> 55.7 us (level)
    ppermute x7 -> x6, starting transfers between devices: 3.43 us -> 3.37 us  [shifted(): lax.ppermute(array, axis, [(i, (i + by) % size) for i in range(size)])]
  transfers between devices with their start and end apart: 22 -> 21, of which waited for: 9 -> 9; matrix products, arithmetic and copies ran while one was open for 0% -> 0% of each run, Pallas kernels for 34% -> 34%
where the time goes in v1:
time: 55.7 us; the launch traced here: 55.5 us
  Pallas kernels  21.7 us (39%)
  starting transfers between devices  20.1 us (36%)
  waiting for transfers between devices  12.8 us (23%)
  between operations  0.82 us (1%)
    pallas_call x12, Pallas kernels, call(): pl.pallas_call(kernel, out_shape=out_shape, in_specs=in_specs or [VMEM] *...  21.7 us
    ppermute x15, starting transfers between devices, crossed(): lax.ppermute(array, axis, [(i, i ^ mask) for i in range(lax.axis_size(axi...  16.7 us
    ppermute x15, waiting for transfers between devices, crossed(): lax.ppermute(array, axis, [(i, i ^ mask) for i in range(lax.axis_size(axi...  12.8 us
    ppermute x6, starting transfers between devices, shifted(): lax.ppermute(array, axis, [(i, (i + by) % size) for i in range(size)])  3.37 us
  transfers between devices with their start and end apart: 21, of which 9 were waited for; matrix products, arithmetic and copies ran while one was open for 0% of the time, Pallas kernels for 34%

profile of v1, /device:TPU:0, one launch (start us, length us, event | category | flops | bytes accessed | tf_op | source)
XLA Modules:
  0.0 55.5 jit_solution(14724471933139484626)
XLA Ops:
  0.6 0.5 collective-permute-start.3
  1.2 3.7 %collective-permute-start.1 = (f32[256,128]{1,0:T(8,128)}, f32[256,128]{1,0:T(8,128)S(1)}, u32[]{:S(2)}, u32[]{:S(2)}) collective-permute-start(f32[256,128]{1,0:T(8,128)} %refs_0_.4), channel_id=1, source_target_pairs={{0,2},{1,3},{2,0},{3,1},{4,6},{5,7},{6,4},{7,5},{8,10},{9,11},{10,... | collective-permute-start | bytes 393224 | tf_op jit(solution)/shard_map/ppermute | solution.py:330
  4.8 1.6 %collective-permute-start = (f32[256,128]{1,0:T(8,128)}, f32[256,128]{1,0:T(8,128)S(1)}, u32[]{:S(2)}, u32[]{:S(2)}) collective-permute-start(f32[256,128]{1,0:T(8,128)} %refs_0_.4), channel_id=1, source_target_pairs={{0,1},{1,0},{2,3},{3,2},{4,5},{5,4},{6,7},{7,6},{8,9},{9,8},{10,11... | collective-permute-start | bytes 393224 | tf_op jit(solution)/shard_map/ppermute | solution.py:330
  6.4 0.0 collective-permute-start.2
  6.4 1.0 %collective-permute-start.4 = (f32[8,128]{1,0:T(8,128)}, f32[8,128]{1,0:T(8,128)S(1)}, u32[]{:S(2)}, u32[]{:S(2)}) collective-permute-start(f32[8,128]{1,0:T(8,128)} %bitcast.1), channel_id=1, source_target_pairs={{0,4},{4,8},{8,12},{12,16},{16,20},{20,24},{24,28},{28,0},{1,5},{5... | collective-permute-start | bytes 12296 | tf_op jit(solution)/shard_map/ppermute | solution.py:326
  7.4 6.2 %shard_map.68 = (f32[1024,128]{1,0:T(8,128)S(1)}, f32[128,128]{1,0:T(8,128)S(1)}, s32[8,128]{1,0:T(8,128)S(1)}, bf16[1024,1024]{1,0:T(8,128)(2,1)S(1)}, bf16[102...) custom-call(s32[8]{0:T(128)} %refs_0_.3, ...), custom_call_target="tpu_custom_call" | custom-call | flops 1610612736 | bytes 4194304 | tf_op jit(solution)/shard_map/pallas_call | solution.py:30
  13.5 0.0 copy-start.1
  13.6 0.0 collective-permute-done.4.row_ref
  13.6 0.0 collective-permute-done.3.factors_ref
  13.6 0.0 copy-start
  13.6 2.9 %shard_map.69 = (f32[1024,128]{1,0:T(8,128)S(1)}, f32[128,128]{1,0:T(8,128)S(1)}) custom-call(f32[1024,128]{1,0:T(8,128)S(1)} %collective-permute-done.3.factors_ref, f32[8,128]{1,0:T(8,128)S(1)} %collective-permute-done.4.row_ref, s32[8,128]{1,0:T(8,128)S(1)} %get-tuple-element.48.bases_ref), custom_call_target="tpu_custom_call" | custom-call | flops 1073741824 | bytes 4194304 | tf_op jit(solution)/shard_map/pallas_call | solution.py:30
  16.5 0.0 collective-permute-done.1.refs_2_
  16.5 0.0 collective-permute-done.refs_1_
  16.5 0.0 collective-permute-done.2.refs_3_
  16.5 0.0 copy-done.1
  16.5 0.5 shard_map.70
  17.0 0.9 %collective-permute-start.5 = (f32[1024,128]{1,0:T(8,128)S(1)}, f32[1024,128]{1,0:T(8,128)S(1)}, u32[]{:S(2)}, u32[]{:S(2)}) collective-permute-start(f32[1024,128]{1,0:T(8,128)S(1)} %get-tuple-element.54), channel_id=1, source_target_pairs={{0,4},{4,8},{8,12},{12,16},{16,20},{20,24},{24,28},{28,0},{1,5},{5... | collective-permute-start | bytes 1572872 | tf_op jit(solution)/shard_map/ppermute | solution.py:326
  17.9 0.0 copy-done
  17.9 1.4 %shard_map.71 = (f32[1024,128]{1,0:T(8,128)S(1)}, f32[16,128]{1,0:T(8,128)S(1)}) custom-call(f32[1024,128]{1,0:T(8,128)S(1)} %copy-done, f32[1024,128]{1,0:T(8,128)S(1)} %get-tuple-element.43.weight_ref, bf16[1024,1024]{1,0:T(8,128)(2,1)S(1)} %get-tuple-element.44.first_ref, bf16[1024,1024]{1,0:T(8,128)(2,1)S(1)} %get-tuple-element.45.second_ref, ...), custom_call_target="tpu_custom_call" | custom-call | flops 1073741824 | bytes 4194304 | tf_op jit(solution)/shard_map/pallas_call | solution.py:30
  19.3 0.8 %collective-permute-start.6 = (f32[16,128]{1,0:T(8,128)S(1)}, f32[16,128]{1,0:T(8,128)S(1)}, u32[]{:S(2)}, u32[]{:S(2)}) collective-permute-start(f32[16,128]{1,0:T(8,128)S(1)} %get-tuple-element.56.sums_ref), channel_id=1, source_target_pairs={{0,4},{4,0},{8,12},{12,8},{16,20},{20,16},{24,28},{28,24},{1,5},{5... | collective-permute-start | bytes 24584 | tf_op jit(solution)/shard_map/ppermute | solution.py:330
  20.2 0.8 %collective-permute-done.6 = f32[16,128]{1,0:T(8,128)S(1)} collective-permute-done((f32[16,128]{1,0:T(8,128)S(1)}, f32[16,128]{1,0:T(8,128)S(1)}, u32[]{:S(2)}, u32[]{:S(2)}) %collective-permute-start.6) | collective-permute-done | bytes 8224 | tf_op jit(solution)/shard_map/ppermute | solution.py:330
  21.0 1.4 %collective-permute-start.9 = (f32[16,128]{1,0:T(8,128)S(1)}, f32[16,128]{1,0:T(8,128)S(1)}, u32[]{:S(2)}, u32[]{:S(2)}) collective-permute-start(f32[16,128]{1,0:T(8,128)S(1)} %add.9.refs_0_.refs_9_), channel_id=1, source_target_pairs={{0,24},{4,28},{8,16},{12,20},{16,8},{20,12},{24,0},{28,4},{1,25},{... | collective-permute-start | bytes 24584 | tf_op jit(solution)/shard_map/ppermute | solution.py:330
  22.4 1.5 %collective-permute-start.8 = (f32[16,128]{1,0:T(8,128)S(1)}, f32[16,128]{1,0:T(8,128)S(1)}, u32[]{:S(2)}, u32[]{:S(2)}) collective-permute-start(f32[16,128]{1,0:T(8,128)S(1)} %add.9.refs_0_.refs_9_), channel_id=1, source_target_pairs={{0,16},{4,20},{8,24},{12,28},{16,0},{20,4},{24,8},{28,12},{1,17},{... | collective-permute-start | bytes 24584 | tf_op jit(solution)/shard_map/ppermute | solution.py:330
  24.0 0.5 collective-permute-start.7
  24.5 1.7 %shard_map.73 = (f32[1024,128]{1,0:T(8,128)S(1)}, f32[128,128]{1,0:T(8,128)S(1)}, f32[128,128]{1,0:T(8,128)S(1)}) custom-call(f32[1024,128]{1,0:T(8,128)S(1)} %copy-done, f32[1024,128]{1,0:T(8,128)S(1)} %get-tuple-element.53.grad_ref.refs_1_, f32[1024,128]{1,0:T(8,128)S(1)} %get-tuple-element.43.weight_ref, ...), custom_call_target="tpu_custom_call" | custom-call | flops 1073741824 | bytes 4194304 | tf_op jit(solution)/shard_map/pallas_call | solution.py:30
  26.2 0.0 collective-permute-done.9.refs_3_.refs_12_
  26.2 0.7 %collective-permute-done.8.refs_2_.refs_11_ = f32[16,128]{1,0:T(8,128)S(1)} collective-permute-done((f32[16,128]{1,0:T(8,128)S(1)}, f32[16,128]{1,0:T(8,128)S(1)}, u32[]{:S(2)}, u32[]{:S(2)}) %collective-permute-start.8) | collective-permute-done | bytes 8224 | tf_op jit(solution)/shard_map/ppermute | solution.py:330
  26.9 0.7 %collective-permute-done.7.refs_1_.refs_10_ = f32[16,128]{1,0:T(8,128)S(1)} collective-permute-done((f32[16,128]{1,0:T(8,128)S(1)}, f32[16,128]{1,0:T(8,128)S(1)}, u32[]{:S(2)}, u32[]{:S(2)}) %collective-permute-start.7) | collective-permute-done | bytes 8224 | tf_op jit(solution)/shard_map/ppermute | solution.py:330
  27.6 0.0 collective-permute-done.5.v_ref
  27.6 0.3 shard_map.72.refs_2_
  27.9 0.2 collective-permute-start.10
  28.2 0.7 %shard_map.74 = (f32[1024,128]{1,0:T(8,128)S(1)}, f32[1024,128]{1,0:T(8,128)S(1)}, f32[8,128]{1,0:T(8,128)S(1)}, bf16[1024,256]{1,0:T(8,128)(2,1)S(1)}, f32[128,128]{1,0:T(8,128)S(1)}) custom-call(f32[1024,128]{1,0:T(8,128)S(1)} %copy-done, f32[1024,128]{1,0:T(8,128)S(1)} %get-tuple-element.53.grad_ref.refs_1_, f32[1024,128]{1,0:T(8,128)S(1)} %shard_map.72.refs_2_, ...), custom_call_target="tpu_custom_call" | custom-call | flops 134217728 | bytes 4194304 | tf_op jit(solution)/shard_map/pallas_call | solution.py:30
  28.9 0.7 %collective-permute-start.11 = (f32[1024,128]{1,0:T(8,128)S(1)}, f32[1024,128]{1,0:T(8,128)S(1)}, u32[]{:S(2)}, u32[]{:S(2)}) collective-permute-start(f32[1024,128]{1,0:T(8,128)S(1)} %get-tuple-element.68), channel_id=1, source_target_pairs={{0,4},{4,8},{8,12},{12,16},{16,20},{20,24},{24,28},{28,0},{1,5},{5... | collective-permute-start | bytes 1572872 | tf_op jit(solution)/shard_map/ppermute | solution.py:326
  29.6 1.4 %shard_map.75 = (f32[1024,128]{1,0:T(8,128)S(1)}, f32[16,128]{1,0:T(8,128)S(1)}) custom-call(f32[1024,128]{1,0:T(8,128)S(1)} %get-tuple-element.63.factors_ref.refs_0_, f32[1024,128]{1,0:T(8,128)S(1)} %get-tuple-element.43.weight_ref, bf16[1024,1024]{1,0:T(8,128)(2,1)S(1)} %get-tuple-element.58.first_ref, ...), custom_call_target="tpu_custom_call" | custom-call | flops 1073741824 | bytes 4194304 | tf_op jit(solution)/shard_map/pallas_call | solution.py:30
  31.0 0.1 collective-permute-start.12
  31.1 1.2 %collective-permute-done.12 = f32[16,128]{1,0:T(8,128)S(1)} collective-permute-done((f32[16,128]{1,0:T(8,128)S(1)}, f32[16,128]{1,0:T(8,128)S(1)}, u32[]{:S(2)}, u32[]{:S(2)}) %collective-permute-start.12) | collective-permute-done | bytes 8224 | tf_op jit(solution)/shard_map/ppermute | solution.py:330
  32.2 2.4 %collective-permute-start.15 = (f32[16,128]{1,0:T(8,128)S(1)}, f32[16,128]{1,0:T(8,128)S(1)}, u32[]{:S(2)}, u32[]{:S(2)}) collective-permute-start(f32[16,128]{1,0:T(8,128)S(1)} %add.10.refs_9_), channel_id=1, source_target_pairs={{0,24},{4,28},{8,16},{12,20},{16,8},{20,12},{24,0},{28,4},{1,25},{... | collective-permute-start | bytes 24584 | tf_op jit(solution)/shard_map/ppermute | solution.py:330
  34.6 0.8 %collective-permute-start.14 = (f32[16,128]{1,0:T(8,128)S(1)}, f32[16,128]{1,0:T(8,128)S(1)}, u32[]{:S(2)}, u32[]{:S(2)}) collective-permute-start(f32[16,128]{1,0:T(8,128)S(1)} %add.10.refs_9_), channel_id=1, source_target_pairs={{0,16},{4,20},{8,24},{12,28},{16,0},{20,4},{24,8},{28,12},{1,17},{... | collective-permute-start | bytes 24584 | tf_op jit(solution)/shard_map/ppermute | solution.py:330
  35.5 0.3 collective-permute-start.13
  35.7 3.4 %shard_map.76 = (f32[1024,128]{1,0:T(8,128)S(1)}, f32[128,128]{1,0:T(8,128)S(1)}, f32[128,128]{1,0:T(8,128)S(1)}, f32[1024,128]{1,0:T(8,128)S(1)}, f32[128,128]{...) custom-call(f32[1024,128]{1,0:T(8,128)S(1)} %get-tuple-element.63.factors_ref.refs_0_, ...), custom_call_target="tpu_custom_call" | custom-call | flops 2147483648 | bytes 4194304 | tf_op jit(solution)/shard_map/pallas_call | solution.py:30
  39.1 0.0 collective-permute-done.15.refs_12_
  39.1 4.6 %collective-permute-done.14.refs_11_ = f32[16,128]{1,0:T(8,128)S(1)} collective-permute-done((f32[16,128]{1,0:T(8,128)S(1)}, f32[16,128]{1,0:T(8,128)S(1)}, u32[]{:S(2)}, u32[]{:S(2)}) %collective-permute-start.14) | collective-permute-done | bytes 8224 | tf_op jit(solution)/shard_map/ppermute | solution.py:330
  43.7 0.0 collective-permute-done.13.refs_10_
  43.7 0.0 collective-permute-done.10.refs_2_
  43.7 0.0 collective-permute-done.11.refs_3_
  43.7 0.8 %shard_map.77 = (f32[1024,128]{1,0:T(8,128)S(1)}, f32[512,128]{1,0:T(8,128)S(1)}, f32[8,128]{1,0:T(8,128)S(1)}, bf16[1024,256]{1,0:T(8,128)(2,1)S(1)}, f32[128,128]{1,0:T(8,128)S(1)}) custom-call(f32[1024,128]{1,0:T(8,128)S(1)} %get-tuple-element.63.factors_ref.refs_0_, f32[1024,128]{1,0:T(8,128)S(1)} %get-tuple-element.67.grad_ref.refs_1_, ...), custom_call_target="tpu_custom_call" | custom-call | flops 134217728 | bytes 4194304 | tf_op jit(solution)/shard_map/pallas_call | solution.py:30
  44.5 0.1 collective-permute-start.16
  44.5 1.5 %shard_map.78 = (f32[1024,128]{1,0:T(8,128)S(1)}, f32[16,128]{1,0:T(8,128)S(1)}) custom-call(f32[1024,128]{1,0:T(8,128)S(1)} %get-tuple-element.75.factors_ref.u_ref, f32[1024,128]{1,0:T(8,128)S(1)} %get-tuple-element.43.weight_ref, bf16[1024,1024]{1,0:T(8,128)(2,1)S(1)} %get-tuple-element.76.first_ref, bf16[1024,1024]{1,0:T(8,128)(2,1)S(1)} %get-tuple-element.77.second_ref, ...), custom_call_target="tpu_custom_call" | custom-call | flops 1073741824 | bytes 4194304 | tf_op jit(solution)/shard_map/pallas_call | solution.py:30
  46.0 0.1 collective-permute-start.17
  46.1 1.2 %collective-permute-done.17 = f32[16,128]{1,0:T(8,128)S(1)} collective-permute-done((f32[16,128]{1,0:T(8,128)S(1)}, f32[16,128]{1,0:T(8,128)S(1)}, u32[]{:S(2)}, u32[]{:S(2)}) %collective-permute-start.17) | collective-permute-done | bytes 8224 | tf_op jit(solution)/shard_map/ppermute | solution.py:330
  47.2 2.7 %collective-permute-start.20 = (f32[16,128]{1,0:T(8,128)S(1)}, f32[16,128]{1,0:T(8,128)S(1)}, u32[]{:S(2)}, u32[]{:S(2)}) collective-permute-start(f32[16,128]{1,0:T(8,128)S(1)} %add.11.refs_0_), channel_id=1, source_target_pairs={{0,24},{4,28},{8,16},{12,20},{16,8},{20,12},{24,0},{28,4},{1,25},{... | collective-permute-start | bytes 24584 | tf_op jit(solution)/shard_map/ppermute | solution.py:330
  49.9 0.8 %collective-permute-start.19 = (f32[16,128]{1,0:T(8,128)S(1)}, f32[16,128]{1,0:T(8,128)S(1)}, u32[]{:S(2)}, u32[]{:S(2)}) collective-permute-start(f32[16,128]{1,0:T(8,128)S(1)} %add.11.refs_0_), channel_id=1, source_target_pairs={{0,16},{4,20},{8,24},{12,28},{16,0},{20,4},{24,8},{28,12},{1,17},{... | collective-permute-start | bytes 24584 | tf_op jit(solution)/shard_map/ppermute | solution.py:330
  50.8 0.0 collective-permute-start.18
  50.8 1.0 %collective-permute-done.20.refs_3_ = f32[16,128]{1,0:T(8,128)S(1)} collective-permute-done((f32[16,128]{1,0:T(8,128)S(1)}, f32[16,128]{1,0:T(8,128)S(1)}, u32[]{:S(2)}, u32[]{:S(2)}) %collective-permute-start.20) | collective-permute-done | bytes 8224 | tf_op jit(solution)/shard_map/ppermute | solution.py:330
  51.8 1.8 %collective-permute-done.19.refs_2_ = f32[16,128]{1,0:T(8,128)S(1)} collective-permute-done((f32[16,128]{1,0:T(8,128)S(1)}, f32[16,128]{1,0:T(8,128)S(1)}, u32[]{:S(2)}, u32[]{:S(2)}) %collective-permute-start.19) | collective-permute-done | bytes 8224 | tf_op jit(solution)/shard_map/ppermute | solution.py:330
  53.6 0.8 %collective-permute-done.18.refs_1_ = f32[16,128]{1,0:T(8,128)S(1)} collective-permute-done((f32[16,128]{1,0:T(8,128)S(1)}, f32[16,128]{1,0:T(8,128)S(1)}, u32[]{:S(2)}, u32[]{:S(2)}) %collective-permute-start.18) | collective-permute-done | bytes 8224 | tf_op jit(solution)/shard_map/ppermute | solution.py:330
  54.4 0.0 collective-permute-done.16.both_ref
  54.4 1.0 %shard_map.79 = (f32[1024,128]{1,0:T(8,128)}, f32[256,128]{1,0:T(8,128)}) custom-call(f32[1024,128]{1,0:T(8,128)S(1)} %get-tuple-element.75.factors_ref.u_ref, f32[1024,128]{1,0:T(8,128)S(1)} %get-tuple-element.81.g_ref, f32[512,128]{1,0:T(8,128)S(1)} %collective-permute-done.16.both_ref, f32[16,128]{1,0:T(8,128)S(1)} %add.11.refs_0_, ...), custom_call_target="tpu_custom_call" | custom-call | bytes 4194304 | tf_op jit(solution)/shard_map/pallas_call | solution.py:30
  (3 shorter events, 0.0 us)
Async XLA Ops:
  0.6 12.9 %collective-permute-start.3 = (f32[1024,128]{1,0:T(8,128)}, f32[1024,128]{1,0:T(8,128)S(1)}, u32[]{:S(2)}, u32[]{:S(2)}) collective-permute-start(f32[1024,128]{1,0:T(8,128)} %refs_0_.5), channel_id=1, source_target_pairs={{0,4},{4,8},{8,12},{12,16},{16,20},{20,24},{24,28},{28,0},{1,5},{5... | collective-permute-start | bytes 1572872 | tf_op jit(solution)/shard_map/ppermute | solution.py:326
  1.2 15.3 %collective-permute-start.1 = (f32[256,128]{1,0:T(8,128)}, f32[256,128]{1,0:T(8,128)S(1)}, u32[]{:S(2)}, u32[]{:S(2)}) collective-permute-start(f32[256,128]{1,0:T(8,128)} %refs_0_.4), channel_id=1, source_target_pairs={{0,2},{1,3},{2,0},{3,1},{4,6},{5,7},{6,4},{7,5},{8,10},{9,11},{10,... | collective-permute-start | bytes 393224 | tf_op jit(solution)/shard_map/ppermute | solution.py:330
  4.8 11.7 %collective-permute-start = (f32[256,128]{1,0:T(8,128)}, f32[256,128]{1,0:T(8,128)S(1)}, u32[]{:S(2)}, u32[]{:S(2)}) collective-permute-start(f32[256,128]{1,0:T(8,128)} %refs_0_.4), channel_id=1, source_target_pairs={{0,1},{1,0},{2,3},{3,2},{4,5},{5,4},{6,7},{7,6},{8,9},{9,8},{10,11... | collective-permute-start | bytes 393224 | tf_op jit(solution)/shard_map/ppermute | solution.py:330
  6.4 10.1 %collective-permute-start.2 = (f32[256,128]{1,0:T(8,128)}, f32[256,128]{1,0:T(8,128)S(1)}, u32[]{:S(2)}, u32[]{:S(2)}) collective-permute-start(f32[256,128]{1,0:T(8,128)} %refs_0_.4), channel_id=1, source_target_pairs={{0,3},{1,2},{2,1},{3,0},{4,7},{5,6},{6,5},{7,4},{8,11},{9,10},{10,... | collective-permute-start | bytes 393224 | tf_op jit(solution)/shard_map/ppermute | solution.py:330
  6.4 7.2 %collective-permute-start.4 = (f32[8,128]{1,0:T(8,128)}, f32[8,128]{1,0:T(8,128)S(1)}, u32[]{:S(2)}, u32[]{:S(2)}) collective-permute-start(f32[8,128]{1,0:T(8,128)} %bitcast.1), channel_id=1, source_target_pairs={{0,4},{4,8},{8,12},{12,16},{16,20},{20,24},{24,28},{28,0},{1,5},{5... | collective-permute-start | bytes 12296 | tf_op jit(solution)/shard_map/ppermute | solution.py:326
  13.5 3.0 %copy-start.1 = (f32[256,128]{1,0:T(8,128)S(1)}, f32[256,128]{1,0:T(8,128)}, u32[]{:S(2)}) copy-start(f32[256,128]{1,0:T(8,128)} %refs_0_.4) | copy-start | bytes 393220
  13.6 4.3 %copy-start = (f32[1024,128]{1,0:T(8,128)S(1)}, f32[1024,128]{1,0:T(8,128)}, u32[]{:S(2)}) copy-start(f32[1024,128]{1,0:T(8,128)} %refs_0_.5) | copy-start | bytes 1572868
  17.0 10.6 %collective-permute-start.5 = (f32[1024,128]{1,0:T(8,128)S(1)}, f32[1024,128]{1,0:T(8,128)S(1)}, u32[]{:S(2)}, u32[]{:S(2)}) collective-permute-start(f32[1024,128]{1,0:T(8,128)S(1)} %get-tuple-element.54), channel_id=1, source_target_pairs={{0,4},{4,8},{8,12},{12,16},{16,20},{20,24},{24,28},{28,0},{1,5},{5... | collective-permute-start | bytes 1572872 | tf_op jit(solution)/shard_map/ppermute | solution.py:326
  19.3 1.7 %collective-permute-start.6 = (f32[16,128]{1,0:T(8,128)S(1)}, f32[16,128]{1,0:T(8,128)S(1)}, u32[]{:S(2)}, u32[]{:S(2)}) collective-permute-start(f32[16,128]{1,0:T(8,128)S(1)} %get-tuple-element.56.sums_ref), channel_id=1, source_target_pairs={{0,4},{4,0},{8,12},{12,8},{16,20},{20,16},{24,28},{28,24},{1,5},{5... | collective-permute-start | bytes 24584 | tf_op jit(solution)/shard_map/ppermute | solution.py:330
  21.0 5.2 %collective-permute-start.9 = (f32[16,128]{1,0:T(8,128)S(1)}, f32[16,128]{1,0:T(8,128)S(1)}, u32[]{:S(2)}, u32[]{:S(2)}) collective-permute-start(f32[16,128]{1,0:T(8,128)S(1)} %add.9.refs_0_.refs_9_), channel_id=1, source_target_pairs={{0,24},{4,28},{8,16},{12,20},{16,8},{20,12},{24,0},{28,4},{1,25},{... | collective-permute-start | bytes 24584 | tf_op jit(solution)/shard_map/ppermute | solution.py:330
  22.4 4.5 %collective-permute-start.8 = (f32[16,128]{1,0:T(8,128)S(1)}, f32[16,128]{1,0:T(8,128)S(1)}, u32[]{:S(2)}, u32[]{:S(2)}) collective-permute-start(f32[16,128]{1,0:T(8,128)S(1)} %add.9.refs_0_.refs_9_), channel_id=1, source_target_pairs={{0,16},{4,20},{8,24},{12,28},{16,0},{20,4},{24,8},{28,12},{1,17},{... | collective-permute-start | bytes 24584 | tf_op jit(solution)/shard_map/ppermute | solution.py:330
  24.0 3.7 %collective-permute-start.7 = (f32[16,128]{1,0:T(8,128)S(1)}, f32[16,128]{1,0:T(8,128)S(1)}, u32[]{:S(2)}, u32[]{:S(2)}) collective-permute-start(f32[16,128]{1,0:T(8,128)S(1)} %add.9.refs_0_.refs_9_), channel_id=1, source_target_pairs={{0,8},{4,12},{8,0},{12,4},{16,24},{20,28},{24,16},{28,20},{1,9},{5... | collective-permute-start | bytes 24584 | tf_op jit(solution)/shard_map/ppermute | solution.py:330
  27.9 15.7 %collective-permute-start.10 = (f32[1024,128]{1,0:T(8,128)S(1)}, f32[1024,128]{1,0:T(8,128)S(1)}, u32[]{:S(2)}, u32[]{:S(2)}) collective-permute-start(f32[1024,128]{1,0:T(8,128)S(1)} %shard_map.72.refs_2_), channel_id=1, source_target_pairs={{0,4},{4,8},{8,12},{12,16},{16,20},{20,24},{24,28},{28,0},{1,5},{5... | collective-permute-start | bytes 1572872 | tf_op jit(solution)/shard_map/ppermute | solution.py:326
  28.9 14.8 %collective-permute-start.11 = (f32[1024,128]{1,0:T(8,128)S(1)}, f32[1024,128]{1,0:T(8,128)S(1)}, u32[]{:S(2)}, u32[]{:S(2)}) collective-permute-start(f32[1024,128]{1,0:T(8,128)S(1)} %get-tuple-element.68), channel_id=1, source_target_pairs={{0,4},{4,8},{8,12},{12,16},{16,20},{20,24},{24,28},{28,0},{1,5},{5... | collective-permute-start | bytes 1572872 | tf_op jit(solution)/shard_map/ppermute | solution.py:326
  31.0 1.2 %collective-permute-start.12 = (f32[16,128]{1,0:T(8,128)S(1)}, f32[16,128]{1,0:T(8,128)S(1)}, u32[]{:S(2)}, u32[]{:S(2)}) collective-permute-start(f32[16,128]{1,0:T(8,128)S(1)} %get-tuple-element.69.sums_ref), channel_id=1, source_target_pairs={{0,4},{4,0},{8,12},{12,8},{16,20},{20,16},{24,28},{28,24},{1,5},{5... | collective-permute-start | bytes 24584 | tf_op jit(solution)/shard_map/ppermute | solution.py:330
  32.2 6.9 %collective-permute-start.15 = (f32[16,128]{1,0:T(8,128)S(1)}, f32[16,128]{1,0:T(8,128)S(1)}, u32[]{:S(2)}, u32[]{:S(2)}) collective-permute-start(f32[16,128]{1,0:T(8,128)S(1)} %add.10.refs_9_), channel_id=1, source_target_pairs={{0,24},{4,28},{8,16},{12,20},{16,8},{20,12},{24,0},{28,4},{1,25},{... | collective-permute-start | bytes 24584 | tf_op jit(solution)/shard_map/ppermute | solution.py:330
  34.6 9.0 %collective-permute-start.14 = (f32[16,128]{1,0:T(8,128)S(1)}, f32[16,128]{1,0:T(8,128)S(1)}, u32[]{:S(2)}, u32[]{:S(2)}) collective-permute-start(f32[16,128]{1,0:T(8,128)S(1)} %add.10.refs_9_), channel_id=1, source_target_pairs={{0,16},{4,20},{8,24},{12,28},{16,0},{20,4},{24,8},{28,12},{1,17},{... | collective-permute-start | bytes 24584 | tf_op jit(solution)/shard_map/ppermute | solution.py:330
  35.5 8.2 %collective-permute-start.13 = (f32[16,128]{1,0:T(8,128)S(1)}, f32[16,128]{1,0:T(8,128)S(1)}, u32[]{:S(2)}, u32[]{:S(2)}) collective-permute-start(f32[16,128]{1,0:T(8,128)S(1)} %add.10.refs_9_), channel_id=1, source_target_pairs={{0,8},{4,12},{8,0},{12,4},{16,24},{20,28},{24,16},{28,20},{1,9},{5... | collective-permute-start | bytes 24584 | tf_op jit(solution)/shard_map/ppermute | solution.py:330
  44.5 9.9 %collective-permute-start.16 = (f32[512,128]{1,0:T(8,128)S(1)}, f32[512,128]{1,0:T(8,128)S(1)}, u32[]{:S(2)}, u32[]{:S(2)}) collective-permute-start(f32[512,128]{1,0:T(8,128)S(1)} %get-tuple-element.82), channel_id=1, source_target_pairs={{0,4},{4,8},{8,12},{12,16},{16,20},{20,24},{24,28},{28,0},{1,5},{5... | collective-permute-start | bytes 786440 | tf_op jit(solution)/shard_map/ppermute | solution.py:326
  46.0 1.2 %collective-permute-start.17 = (f32[16,128]{1,0:T(8,128)S(1)}, f32[16,128]{1,0:T(8,128)S(1)}, u32[]{:S(2)}, u32[]{:S(2)}) collective-permute-start(f32[16,128]{1,0:T(8,128)S(1)} %get-tuple-element.83), channel_id=1, source_target_pairs={{0,4},{4,0},{8,12},{12,8},{16,20},{20,16},{24,28},{28,24},{1,5},{5... | collective-permute-start | bytes 24584 | tf_op jit(solution)/shard_map/ppermute | solution.py:330
  47.2 4.5 %collective-permute-start.20 = (f32[16,128]{1,0:T(8,128)S(1)}, f32[16,128]{1,0:T(8,128)S(1)}, u32[]{:S(2)}, u32[]{:S(2)}) collective-permute-start(f32[16,128]{1,0:T(8,128)S(1)} %add.11.refs_0_), channel_id=1, source_target_pairs={{0,24},{4,28},{8,16},{12,20},{16,8},{20,12},{24,0},{28,4},{1,25},{... | collective-permute-start | bytes 24584 | tf_op jit(solution)/shard_map/ppermute | solution.py:330
  49.9 3.7 %collective-permute-start.19 = (f32[16,128]{1,0:T(8,128)S(1)}, f32[16,128]{1,0:T(8,128)S(1)}, u32[]{:S(2)}, u32[]{:S(2)}) collective-permute-start(f32[16,128]{1,0:T(8,128)S(1)} %add.11.refs_0_), channel_id=1, source_target_pairs={{0,16},{4,20},{8,24},{12,28},{16,0},{20,4},{24,8},{28,12},{1,17},{... | collective-permute-start | bytes 24584 | tf_op jit(solution)/shard_map/ppermute | solution.py:330
  50.8 3.7 %collective-permute-start.18 = (f32[16,128]{1,0:T(8,128)S(1)}, f32[16,128]{1,0:T(8,128)S(1)}, u32[]{:S(2)}, u32[]{:S(2)}) collective-permute-start(f32[16,128]{1,0:T(8,128)S(1)} %add.11.refs_0_), channel_id=1, source_target_pairs={{0,8},{4,12},{8,0},{12,4},{16,24},{20,28},{24,16},{28,20},{1,9},{5... | collective-permute-start | bytes 24584 | tf_op jit(solution)/shard_map/ppermute | solution.py:330
